TPU v7x, 256 devices: a whole 4x4x8 slice. The times are simulated.
256 devices in a mesh: mp: 32 (over z, y_hi, core), dp: 8 (over x, y_lo).
Axes of the slice: x: 4, y: 4 (y_hi: 2, y_lo: 2; y = y_hi * 2 + y_lo), z: 8, core: 2. Of those that a mesh axis runs over, the one named last changes fastest.
Arguments:
- tokens: bfloat16 [1024, 8192], P('mp', 'dp'), may hold values from -6 to 6
- gate_weight: bfloat16 [8192, 16384], P('dp', 'mp'), may hold values from -0.0625 to 0.0625
- up_weight: bfloat16 [8192, 16384], P('dp', 'mp'), may hold values from -0.0625 to 0.0625
- down_weight: bfloat16 [16384, 8192], P('mp', 'dp'), may hold values from -0.046875 to 0.046875
- cotangent: bfloat16 [1024, 8192], P('mp', 'dp'), may hold values from -6 to 6
Outputs:
- mixed: bfloat16 [1024, 8192], P('mp', 'dp')
- token_grad: bfloat16 [1024, 8192], P('mp', 'dp')
- gate_grad: bfloat16 [8192, 16384], P('dp', 'mp')
- up_grad: bfloat16 [8192, 16384], P('dp', 'mp')
- down_grad: bfloat16 [16384, 8192], P('mp', 'dp')
All inputs are finite; a program needn't handle non-finite values.
Results may differ from a plain program's by a relative error of at most 0.005.
Values may be sent and summed in bfloat16 or wider, within the bound.
No kernel may reach another device: no remote copies, remote signals or barrier semaphores. Data moves between devices by JAX's collectives and lax.ppermute only.
A program may use at most 64 MiB of HBM per device.

v0:
```python
import jax
import jax.numpy as jnp
from jax import lax
from jax.sharding import Mesh, PartitionSpec as P


f32 = jnp.float32
bf16 = jnp.bfloat16

SWAP = [(0, 1), (1, 0)]
RING = ([(0, 1), (1, 0), (2, 3), (3, 2)], [(0, 3), (3, 0), (1, 2), (2, 1)])


def swap(value, axis):
    return lax.ppermute(value, axis, SWAP)


def across(value, dim):
    if dim == "c":
        return lax.ppermute(value, "yl", SWAP)
    pairs = [(4 * c + i, 4 * c + j) for c in range(2) for i, j in RING[c if dim == "p" else 1 - c]]
    return lax.ppermute(value, ("core", "x"), pairs)


def dot(left, right):
    return jnp.dot(left, right, preferred_element_type=f32)


def dot_rows(left, right):
    return lax.dot_general(left, right, (((0,), (0,)), ((), ())), preferred_element_type=f32)


def dot_cols(left, right):
    return lax.dot_general(left, right, (((1,), (1,)), ((), ())), preferred_element_type=f32)


def along_z(value, by):
    pairs = [(2 * z + c, 2 * ((z + (by if c == 0 else -by)) % 8) + c) for z in range(8) for c in range(2)]
    return lax.ppermute(value, ("z", "core"), pairs)


def join(*parts):
    return jnp.concatenate(parts, axis=0)


def gather_mp(own, first=None):
    pair = join(own, swap(own, "core"))
    near = along_z(pair, 1)
    far = along_z(own, 4)
    pairs = along_z(join(pair, near), 2)
    quarter = join(own, near, pairs, far)
    other = swap(quarter, "yh")
    if first is not None:
        other = after(other, first)
    return join(quarter, other)


def scatter_yh(total):
    return total[:256] + swap(total[256:].astype(bf16), "yh").astype(f32)


def scatter_z(total, *first):
    pairs = after(along_z(total[96:224].astype(bf16), -2), *first).astype(f32)
    far = along_z(total[224:].astype(bf16), 4).astype(f32)
    near = along_z((total[32:96] + pairs[64:]).astype(bf16), -1).astype(f32)
    last = swap(pairs[32:64] + near[32:], "core")
    return (total[:32] + far + pairs[:32] + near[:32] + last).astype(bf16)


def after(value, *others):
    return lax.optimization_barrier((value,) + others)[0]


def rows(value, start, size):
    return lax.dynamic_slice_p.bind(value, start, jnp.int32(0), slice_sizes=(size, value.shape[1]))


def scatter_dp(left, product, bits):
    keep, size, sent = left, 512, None
    for dim in "pqc":
        size //= 2
        mine, other, _ = bits[dim]
        kind = f32 if dim == "c" else bf16
        send = product(rows(keep, other, size)).astype(kind)
        sent = send if sent is None else sent
        got = across(send, dim)
        keep = product(rows(keep, mine, size)) + got.astype(f32)
        product = lambda block: block
    return keep, sent


def gather_dp(share, bits, first=None):
    for dim in "cqp":
        other = across(share, dim)
        if first is not None and dim == "q":
            other = after(other, first)
        share = jnp.where(bits[dim][2], join(share, other), join(other, share))
    return share


def body(tokens, gate_weight, up_weight, down_weight, cotangent):
    x, core = lax.axis_index("x"), lax.axis_index("core")
    first, second = (x ^ (x >> 1)) & 1, x >> 1
    bits = {"p": jnp.where(core == 0, first, second), "q": jnp.where(core == 0, second, first), "c": lax.axis_index("yl")}
    bits = {dim: (bits[dim] * size, size - bits[dim] * size, bits[dim] == 0) for dim, size in (("p", 256), ("q", 128), ("c", 64))}
    tokens, cotangent, bits = lax.optimization_barrier((tokens, cotangent, bits))

    width = gate_weight.shape[1]
    own_weights = jnp.concatenate([gate_weight, up_weight], axis=1)
    both_weights = jnp.concatenate([own_weights, swap(own_weights, "core")], axis=1)
    down_weights = join(down_weight, swap(down_weight, "core"))

    depth = tokens.shape[1]
    token_half = gather_mp(tokens)
    both, sent = scatter_dp(token_half, lambda block: dot(block, both_weights), bits)
    cot_half = gather_mp(cotangent, sent)
    hidden_back, _ = scatter_dp(cot_half, lambda block: dot_cols(block, down_weights), bits)

    gate = jnp.concatenate([both[:, :width], both[:, 2 * width : 3 * width]], axis=1)
    up = jnp.concatenate([both[:, width : 2 * width], both[:, 3 * width :]], axis=1)
    hidden = (gate * jax.nn.sigmoid(gate) * up).astype(bf16)
    hidden, gate, up = lax.optimization_barrier((hidden, gate, up))
    sig = jax.nn.sigmoid(gate)
    act = gate * sig
    pre_gate = (hidden_back * up * sig * (1.0 + gate * (1.0 - sig))).astype(bf16)
    pre_up = (hidden_back * act).astype(bf16)
    pre = jnp.concatenate(
        [pre_gate[:, :width], pre_up[:, :width], pre_gate[:, width:], pre_up[:, width:]], axis=1
    )
    hidden_half = gather_dp(hidden, bits, pre)
    pre_half = gather_dp(pre, bits)

    token_other, cot_other = swap(token_half, "core"), swap(cot_half, "core")
    hidden_other = swap(hidden_half[:, width:], "core")
    pre_other = swap(pre_half[:, 2 * width :], "core")
    down_grad = (dot_rows(hidden_half[:, :width], cot_half) + dot_rows(hidden_other, cot_other)).astype(bf16)
    grads = (dot_rows(token_half, pre_half[:, : 2 * width]) + dot_rows(token_other, pre_other)).astype(bf16)

    mixed = scatter_yh(dot(hidden_half, down_weights))
    token_grad = scatter_yh(dot_cols(pre_half, both_weights))
    out = scatter_z(jnp.concatenate([mixed, token_grad], axis=1), grads, down_grad)
    return (out[:, :depth], out[:, depth:], grads[:, :width], grads[:, width:], down_grad)


def solution(mesh):
    fine = Mesh(mesh.devices.reshape(8, 2, 2, 4, 2), ("z", "yh", "core", "x", "yl"))
    mp, dp = ("z", "yh", "core"), ("x", "yl")
    in_specs = (P(mp, dp), P(dp, mp), P(dp, mp), P(mp, dp), P(mp, dp))
    out_specs = (P(mp, dp), P(mp, dp), P(dp, mp), P(dp, mp), P(mp, dp))
    return jax.shard_map(body, mesh=fine, in_specs=in_specs, out_specs=out_specs, check_vma=False)
```

profile of v0, /device:TPU:6, one launch (start us, length us, event | category | flops | bytes accessed | tf_op | source)
XLA Modules:
  0.0 179.6 jit_solution(718752695204144181)
XLA Ops:
  0.7 3.3 %pad_maximum_fusion.1 = bf16[1024,1024]{1,0:T(8,128)(2,1)} fusion(bf16[1024,512]{1,0:T(8,128)(2,1)} %param.7, bf16[1024,512]{1,0:T(8,128)(2,1)} %param.6), kind=kLoop, calls=%fused_computation.9 | loop fusion | flops 4194304 | bytes 4194304 | tf_op jit(solution)/shard_map/concatenate | solution.py:109
  4.4 7.2 %collective-permute-start.3 = (bf16[32,1024]{1,0:T(8,128)(2,1)S(1)}, bf16[32,1024]{1,0:T(8,128)(2,1)S(1)}, u32[]{:S(2)}, u32[]{:S(2)}) collective-permute-start(bf16[32,1024]{1,0:T(8,128)(2,1)S(1)} %copy-done.3), channel_id=1, source_target_pairs={{0,128},{8,136},{32,160},{40,168},{64,192},{72,200},{96,224},{104,... | collective-permute-start | bytes 196616 | tf_op jit(solution)/shard_map/ppermute | solution.py:39
  13.4 5.0 %collective-permute-done.1 = bf16[64,1024]{1,0:T(8,128)(2,1)S(1)} collective-permute-done((bf16[64,1024]{1,0:T(8,128)(2,1)S(1)}, bf16[64,1024]{1,0:T(8,128)(2,1)S(1)}, u32[]{:S(2)}, u32[]{:S(2)}) %collective-permute-start.1) | collective-permute-done | bytes 131104 | tf_op jit(solution)/shard_map/ppermute | solution.py:39
  19.2 3.9 %collective-permute-start.14 = (bf16[32,1024]{1,0:T(8,128)(2,1)S(1)}, bf16[32,1024]{1,0:T(8,128)(2,1)S(1)}, u32[]{:S(2)}, u32[]{:S(2)}) collective-permute-start(bf16[32,1024]{1,0:T(8,128)(2,1)S(1)} %copy-done.4), channel_id=1, source_target_pairs={{0,128},{8,136},{32,160},{40,168},{64,192},{72,200},{96,224},{104,... | collective-permute-start | bytes 196616 | tf_op jit(solution)/shard_map/ppermute | solution.py:39
  23.6 6.3 %collective-permute-done.2 = bf16[128,1024]{1,0:T(8,128)(2,1)S(1)} collective-permute-done((bf16[128,1024]{1,0:T(8,128)(2,1)S(1)}, bf16[128,1024]{1,0:T(8,128)(2,1)S(1)}, u32[]{:S(2)}, u32[]{:S(2)}) %collective-permute-start.2) | collective-permute-done | bytes 262176 | tf_op jit(solution)/shard_map/ppermute | solution.py:39
  30.0 3.3 %collective-permute-start.4 = (bf16[256,1024]{1,0:T(8,128)(2,1)S(1)}, bf16[256,1024]{1,0:T(8,128)(2,1)S(1)}, u32[]{:S(2)}, u32[]{:S(2)}) collective-permute-start(bf16[256,1024]{1,0:T(8,128)(2,1)S(1)} %pad_maximum_fusion.2), channel_id=1, source_target_pairs={{0,16},{16,0},{1,17},{17,1},{2,18},{18,2},{3,19},{19,3},{4,20},{20... | collective-permute-start | bytes 1572872 | tf_op jit(solution)/shard_map/ppermute | solution.py:15
  34.1 7.9 %collective-permute-done.4 = bf16[256,1024]{1,0:T(8,128)(2,1)S(1)} collective-permute-done((bf16[256,1024]{1,0:T(8,128)(2,1)S(1)}, bf16[256,1024]{1,0:T(8,128)(2,1)S(1)}, u32[]{:S(2)}, u32[]{:S(2)}) %collective-permute-start.4) | collective-permute-done | bytes 524320 | tf_op jit(solution)/shard_map/ppermute | solution.py:15
  44.5 3.3 %collective-permute-start.15 = (bf16[256,1024]{1,0:T(8,128)(2,1)S(1)}, bf16[256,1024]{1,0:T(8,128)(2,1)S(1)}, u32[]{:S(2)}, u32[]{:S(2)}) collective-permute-start(bf16[256,1024]{1,0:T(8,128)(2,1)S(1)} %pad_maximum_fusion.3), channel_id=1, source_target_pairs={{0,16},{16,0},{1,17},{17,1},{2,18},{18,2},{3,19},{19,3},{4,20},{20... | collective-permute-start | bytes 1572872 | tf_op jit(solution)/shard_map/ppermute | solution.py:15
  47.9 7.5 %collective-permute-done.15 = bf16[256,1024]{1,0:T(8,128)(2,1)S(1)} collective-permute-done((bf16[256,1024]{1,0:T(8,128)(2,1)S(1)}, bf16[256,1024]{1,0:T(8,128)(2,1)S(1)}, u32[]{:S(2)}, u32[]{:S(2)}) %collective-permute-start.15) | collective-permute-done | bytes 524320 | tf_op jit(solution)/shard_map/ppermute | solution.py:15
  60.7 10.7 %collective-permute-done.17 = bf16[256,1024]{1,0:T(8,128)(2,1)S(1)} collective-permute-done((bf16[256,1024]{1,0:T(8,128)(2,1)S(1)}, bf16[256,1024]{1,0:T(8,128)(2,1)S(1)}, u32[]{:S(2)}, u32[]{:S(2)}) %collective-permute-start.17) | collective-permute-done | bytes 524320 | tf_op jit(solution)/shard_map/ppermute | solution.py:22
  72.3 1.7 collective-permute-start.18
  74.2 2.2 %collective-permute-start.8 = (f32[64,2048]{1,0:T(8,128)S(1)}, f32[64,2048]{1,0:T(8,128)S(1)}, u32[]{:S(2)}, u32[]{:S(2)}) collective-permute-start(f32[64,2048]{1,0:T(8,128)S(1)} %constant_dynamic-slice_fusion.1), channel_id=1, source_target_pairs={{0,1},{1,0},{2,3},{3,2},{4,5},{5,4},{6,7},{7,6},{8,9},{9,8},{10,11... | collective-permute-start | bytes 1572872 | tf_op jit(solution)/shard_map/ppermute | solution.py:20
  76.5 3.5 %collective-permute-done.18 = bf16[128,1024]{1,0:T(8,128)(2,1)S(1)} collective-permute-done((bf16[128,1024]{1,0:T(8,128)(2,1)S(1)}, bf16[128,1024]{1,0:T(8,128)(2,1)S(1)}, u32[]{:S(2)}, u32[]{:S(2)}) %collective-permute-start.18) | collective-permute-done | bytes 262176 | tf_op jit(solution)/shard_map/ppermute | solution.py:22
  80.1 2.2 %collective-permute-start.19 = (f32[64,1024]{1,0:T(8,128)S(1)}, f32[64,1024]{1,0:T(8,128)S(1)}, u32[]{:S(2)}, u32[]{:S(2)}) collective-permute-start(f32[64,1024]{1,0:T(8,128)S(1)} %constant_dynamic-slice_fusion), channel_id=1, source_target_pairs={{0,1},{1,0},{2,3},{3,2},{4,5},{5,4},{6,7},{7,6},{8,9},{9,8},{10,11... | collective-permute-start | bytes 786440 | tf_op jit(solution)/shard_map/ppermute | solution.py:20
  82.3 3.9 %collective-permute-done.8 = f32[64,2048]{1,0:T(8,128)S(1)} collective-permute-done((f32[64,2048]{1,0:T(8,128)S(1)}, f32[64,2048]{1,0:T(8,128)S(1)}, u32[]{:S(2)}, u32[]{:S(2)}) %collective-permute-start.8) | collective-permute-done | bytes 524320 | tf_op jit(solution)/shard_map/ppermute | solution.py:20
  86.5 5.4 %collective-permute-done.19 = f32[64,1024]{1,0:T(8,128)S(1)} collective-permute-done((f32[64,1024]{1,0:T(8,128)S(1)}, f32[64,1024]{1,0:T(8,128)S(1)}, u32[]{:S(2)}, u32[]{:S(2)}) %collective-permute-start.19) | collective-permute-done | bytes 262176 | tf_op jit(solution)/shard_map/ppermute | solution.py:20
  92.1 1.8 collective-permute-start.22
  94.2 5.8 %collective-permute-done.9 = bf16[64,1024]{1,0:T(8,128)(2,1)S(1)} collective-permute-done((bf16[64,1024]{1,0:T(8,128)(2,1)S(1)}, bf16[64,1024]{1,0:T(8,128)(2,1)S(1)}, u32[]{:S(2)}, u32[]{:S(2)}) %collective-permute-start.9) | collective-permute-done | bytes 131104 | tf_op jit(solution)/shard_map/ppermute | solution.py:20
  100.6 2.9 %collective-permute-start.23 = (bf16[128,2048]{1,0:T(8,128)(2,1)S(1)}, bf16[128,2048]{1,0:T(8,128)(2,1)S(1)}, u32[]{:S(2)}, u32[]{:S(2)}) collective-permute-start(bf16[128,2048]{1,0:T(8,128)(2,1)S(1)} %maximum_select_fusion.4), channel_id=1, source_target_pairs={{0,6},{6,0},{2,4},{4,2},{8,10},{10,8},{12,14},{14,12},{1,7},{7,1},... | collective-permute-start | bytes 1572872 | tf_op jit(solution)/shard_map/ppermute | solution.py:22
  103.5 7.0 %collective-permute-done.10 = bf16[128,1024]{1,0:T(8,128)(2,1)S(1)} collective-permute-done((bf16[128,1024]{1,0:T(8,128)(2,1)S(1)}, bf16[128,1024]{1,0:T(8,128)(2,1)S(1)}, u32[]{:S(2)}, u32[]{:S(2)}) %collective-permute-start.10) | collective-permute-done | bytes 262176 | tf_op jit(solution)/shard_map/ppermute | solution.py:22
  110.8 5.9 %collective-permute-done.23 = bf16[128,2048]{1,0:T(8,128)(2,1)S(1)} collective-permute-done((bf16[128,2048]{1,0:T(8,128)(2,1)S(1)}, bf16[128,2048]{1,0:T(8,128)(2,1)S(1)}, u32[]{:S(2)}, u32[]{:S(2)}) %collective-permute-start.23) | collective-permute-done | bytes 524320 | tf_op jit(solution)/shard_map/ppermute | solution.py:22
  117.1 2.8 %collective-permute-done.20 = bf16[256,1024]{1,0:T(8,128)(2,1)S(1)} collective-permute-done((bf16[256,1024]{1,0:T(8,128)(2,1)S(1)}, bf16[256,1024]{1,0:T(8,128)(2,1)S(1)}, u32[]{:S(2)}, u32[]{:S(2)}) %collective-permute-start.20) | collective-permute-done | bytes 524320 | tf_op jit(solution)/shard_map/ppermute | solution.py:22
  122.3 3.2 %collective-permute-start.21 = (bf16[256,1024]{1,0:T(8,128)(2,1)S(1)}, bf16[256,1024]{1,0:T(8,128)(2,1)S(1)}, u32[]{:S(2)}, u32[]{:S(2)}) collective-permute-start(bf16[256,1024]{1,0:T(8,128)(2,1)S(1)} %slice.197), channel_id=1, source_target_pairs={{0,16},{16,0},{1,17},{17,1},{2,18},{18,2},{3,19},{19,3},{4,20},{20... | collective-permute-start | bytes 1572872 | tf_op jit(solution)/shard_map/ppermute | solution.py:15
  126.3 5.6 %collective-permute-done.24 = bf16[256,2048]{1,0:T(8,128)(2,1)S(1)} collective-permute-done((bf16[256,2048]{1,0:T(8,128)(2,1)S(1)}, bf16[256,2048]{1,0:T(8,128)(2,1)S(1)}, u32[]{:S(2)}, u32[]{:S(2)}) %collective-permute-start.24) | collective-permute-done | bytes 1048608 | tf_op jit(solution)/shard_map/ppermute | solution.py:22
  133.0 2.4 %fusion.26 = f32[512,1024]{1,0:T(8,128)S(1)} fusion(bf16[512,2048]{1,0:T(8,128)(2,1)S(1)} %maximum_select_fusion, bf16[1024,2048]{1,0:T(8,128)(2,1)S(1)} %constant_dynamic-update-slice_fusion.5), kind=kOutput, calls=%fused_computation.85 | convolution fusion | flops 2147483648 | bytes 8388608 | tf_op jit(solution)/shard_map/dot_general | solution.py:34
  135.4 3.5 %collective-permute-start.25 = (bf16[256,1024]{1,0:T(8,128)(2,1)S(1)}, bf16[256,1024]{1,0:T(8,128)(2,1)S(1)}, u32[]{:S(2)}, u32[]{:S(2)}) collective-permute-start(bf16[256,1024]{1,0:T(8,128)(2,1)S(1)} %slice.196), channel_id=1, source_target_pairs={{0,16},{16,0},{1,17},{17,1},{2,18},{18,2},{3,19},{19,3},{4,20},{20... | collective-permute-start | bytes 1572872 | tf_op jit(solution)/shard_map/ppermute | solution.py:15
  139.1 1.7 add_convert_fusion.1
  140.8 8.5 %collective-permute-done.25 = bf16[256,1024]{1,0:T(8,128)(2,1)S(1)} collective-permute-done((bf16[256,1024]{1,0:T(8,128)(2,1)S(1)}, bf16[256,1024]{1,0:T(8,128)(2,1)S(1)}, u32[]{:S(2)}, u32[]{:S(2)}) %collective-permute-start.25) | collective-permute-done | bytes 524320 | tf_op jit(solution)/shard_map/ppermute | solution.py:15
  152.5 7.3 %collective-permute-done.27 = bf16[128,2048]{1,0:T(8,128)(2,1)S(1)} collective-permute-done((bf16[128,2048]{1,0:T(8,128)(2,1)S(1)}, bf16[128,2048]{1,0:T(8,128)(2,1)S(1)}, u32[]{:S(2)}, u32[]{:S(2)}) %collective-permute-start.27) | collective-permute-done | bytes 524320 | tf_op jit(solution)/shard_map/ppermute | solution.py:39
  160.0 9.9 %collective-permute-start.32 = (bf16[64,2048]{1,0:T(8,128)(2,1)S(1)}, bf16[64,2048]{1,0:T(8,128)(2,1)S(1)}, u32[]{:S(2)}, u32[]{:S(2)}) collective-permute-start(bf16[64,2048]{1,0:T(8,128)(2,1)S(1)} %fusion.4), channel_id=1, source_target_pairs={{0,224},{8,40},{32,0},{40,72},{64,32},{72,104},{96,64},{104,136},{... | collective-permute-start | bytes 786440 | tf_op jit(solution)/shard_map/ppermute | solution.py:39
  169.9 1.7 collective-permute-start.26
  171.6 4.3 %collective-permute-done.32 = bf16[64,2048]{1,0:T(8,128)(2,1)S(1)} collective-permute-done((bf16[64,2048]{1,0:T(8,128)(2,1)S(1)}, bf16[64,2048]{1,0:T(8,128)(2,1)S(1)}, u32[]{:S(2)}, u32[]{:S(2)}) %collective-permute-start.32) | collective-permute-done | bytes 262176 | tf_op jit(solution)/shard_map/ppermute | solution.py:39
  (112 shorter events, 27.0 us)
Async XLA Ops:
  3.9 38.1 %collective-permute-start.5 = (bf16[1024,1024]{1,0:T(8,128)(2,1)}, bf16[1024,1024]{1,0:T(8,128)(2,1)S(1)}, u32[]{:S(2)}, u32[]{:S(2)}) collective-permute-start(bf16[1024,1024]{1,0:T(8,128)(2,1)} %pad_maximum_fusion.1), channel_id=1, source_target_pairs={{0,8},{8,0},{1,9},{9,1},{2,10},{10,2},{3,11},{11,3},{4,12},{12,4},... | collective-permute-start | bytes 6291464 | tf_op jit(solution)/shard_map/ppermute | solution.py:15
  3.9 8.2 %collective-permute-start = (bf16[32,1024]{1,0:T(8,128)(2,1)S(1)}, bf16[32,1024]{1,0:T(8,128)(2,1)S(1)}, u32[]{:S(2)}, u32[]{:S(2)}) collective-permute-start(bf16[32,1024]{1,0:T(8,128)(2,1)S(1)} %copy-done.3), channel_id=1, source_target_pairs={{0,8},{8,0},{1,9},{9,1},{2,10},{10,2},{3,11},{11,3},{4,12},{12,4},... | collective-permute-start | bytes 196616 | tf_op jit(solution)/shard_map/ppermute | solution.py:15
  4.4 18.7 %collective-permute-start.3 = (bf16[32,1024]{1,0:T(8,128)(2,1)S(1)}, bf16[32,1024]{1,0:T(8,128)(2,1)S(1)}, u32[]{:S(2)}, u32[]{:S(2)}) collective-permute-start(bf16[32,1024]{1,0:T(8,128)(2,1)S(1)} %copy-done.3), channel_id=1, source_target_pairs={{0,128},{8,136},{32,160},{40,168},{64,192},{72,200},{96,224},{104,... | collective-permute-start | bytes 196616 | tf_op jit(solution)/shard_map/ppermute | solution.py:39
  11.6 36.2 %collective-permute-start.16 = (bf16[512,1024]{1,0:T(8,128)(2,1)}, bf16[512,1024]{1,0:T(8,128)(2,1)S(1)}, u32[]{:S(2)}, u32[]{:S(2)}) collective-permute-start(bf16[512,1024]{1,0:T(8,128)(2,1)} %param.8), channel_id=1, source_target_pairs={{0,8},{8,0},{1,9},{9,1},{2,10},{10,2},{3,11},{11,3},{4,12},{12,4},... | collective-permute-start | bytes 3145736 | tf_op jit(solution)/shard_map/ppermute | solution.py:15
  11.6 7.6 %collective-permute-start.11 = (bf16[32,1024]{1,0:T(8,128)(2,1)S(1)}, bf16[32,1024]{1,0:T(8,128)(2,1)S(1)}, u32[]{:S(2)}, u32[]{:S(2)}) collective-permute-start(bf16[32,1024]{1,0:T(8,128)(2,1)S(1)} %copy-done.4), channel_id=1, source_target_pairs={{0,8},{8,0},{1,9},{9,1},{2,10},{10,2},{3,11},{11,3},{4,12},{12,4},... | collective-permute-start | bytes 196616 | tf_op jit(solution)/shard_map/ppermute | solution.py:15
  12.2 6.3 %collective-permute-start.1 = (bf16[64,1024]{1,0:T(8,128)(2,1)S(1)}, bf16[64,1024]{1,0:T(8,128)(2,1)S(1)}, u32[]{:S(2)}, u32[]{:S(2)}) collective-permute-start(bf16[64,1024]{1,0:T(8,128)(2,1)S(1)} %pad_maximum_fusion.9), channel_id=1, source_target_pairs={{0,32},{8,232},{32,64},{40,8},{64,96},{72,40},{96,128},{104,72},{1... | collective-permute-start | bytes 393224 | tf_op jit(solution)/shard_map/ppermute | solution.py:39
  18.4 11.5 %collective-permute-start.2 = (bf16[128,1024]{1,0:T(8,128)(2,1)S(1)}, bf16[128,1024]{1,0:T(8,128)(2,1)S(1)}, u32[]{:S(2)}, u32[]{:S(2)}) collective-permute-start(bf16[128,1024]{1,0:T(8,128)(2,1)S(1)} %pad_maximum_fusion.4), channel_id=1, source_target_pairs={{0,64},{8,200},{32,96},{40,232},{64,128},{72,8},{96,160},{104,40},... | collective-permute-start | bytes 786440 | tf_op jit(solution)/shard_map/ppermute | solution.py:39
  19.2 25.3 %collective-permute-start.14 = (bf16[32,1024]{1,0:T(8,128)(2,1)S(1)}, bf16[32,1024]{1,0:T(8,128)(2,1)S(1)}, u32[]{:S(2)}, u32[]{:S(2)}) collective-permute-start(bf16[32,1024]{1,0:T(8,128)(2,1)S(1)} %copy-done.4), channel_id=1, source_target_pairs={{0,128},{8,136},{32,160},{40,168},{64,192},{72,200},{96,224},{104,... | collective-permute-start | bytes 196616 | tf_op jit(solution)/shard_map/ppermute | solution.py:39
  23.1 10.1 %collective-permute-start.12 = (bf16[64,1024]{1,0:T(8,128)(2,1)S(1)}, bf16[64,1024]{1,0:T(8,128)(2,1)S(1)}, u32[]{:S(2)}, u32[]{:S(2)}) collective-permute-start(bf16[64,1024]{1,0:T(8,128)(2,1)S(1)} %pad_maximum_fusion.10), channel_id=1, source_target_pairs={{0,32},{8,232},{32,64},{40,8},{64,96},{72,40},{96,128},{104,72},{1... | collective-permute-start | bytes 393224 | tf_op jit(solution)/shard_map/ppermute | solution.py:39
  30.0 12.0 %collective-permute-start.4 = (bf16[256,1024]{1,0:T(8,128)(2,1)S(1)}, bf16[256,1024]{1,0:T(8,128)(2,1)S(1)}, u32[]{:S(2)}, u32[]{:S(2)}) collective-permute-start(bf16[256,1024]{1,0:T(8,128)(2,1)S(1)} %pad_maximum_fusion.2), channel_id=1, source_target_pairs={{0,16},{16,0},{1,17},{17,1},{2,18},{18,2},{3,19},{19,3},{4,20},{20... | collective-permute-start | bytes 1572872 | tf_op jit(solution)/shard_map/ppermute | solution.py:15
  33.3 11.2 %collective-permute-start.13 = (bf16[128,1024]{1,0:T(8,128)(2,1)S(1)}, bf16[128,1024]{1,0:T(8,128)(2,1)S(1)}, u32[]{:S(2)}, u32[]{:S(2)}) collective-permute-start(bf16[128,1024]{1,0:T(8,128)(2,1)S(1)} %pad_maximum_fusion.7), channel_id=1, source_target_pairs={{0,64},{8,200},{32,96},{40,232},{64,128},{72,8},{96,160},{104,40},... | collective-permute-start | bytes 786440 | tf_op jit(solution)/shard_map/ppermute | solution.py:39
  43.6 14.9 %collective-permute-start.6 = (bf16[256,2048]{1,0:T(8,128)(2,1)S(1)}, bf16[256,2048]{1,0:T(8,128)(2,1)S(1)}, u32[]{:S(2)}, u32[]{:S(2)}) collective-permute-start(bf16[256,2048]{1,0:T(8,128)(2,1)S(1)} %convolution_convert_fusion), channel_id=1, source_target_pairs={{0,2},{2,0},{4,6},{6,4},{8,14},{14,8},{10,12},{12,10},{1,3},{3,1},... | collective-permute-start | bytes 3145736 | tf_op jit(solution)/shard_map/ppermute | solution.py:22
  44.5 11.0 %collective-permute-start.15 = (bf16[256,1024]{1,0:T(8,128)(2,1)S(1)}, bf16[256,1024]{1,0:T(8,128)(2,1)S(1)}, u32[]{:S(2)}, u32[]{:S(2)}) collective-permute-start(bf16[256,1024]{1,0:T(8,128)(2,1)S(1)} %pad_maximum_fusion.3), channel_id=1, source_target_pairs={{0,16},{16,0},{1,17},{17,1},{2,18},{18,2},{3,19},{19,3},{4,20},{20... | collective-permute-start | bytes 1572872 | tf_op jit(solution)/shard_map/ppermute | solution.py:15
  56.3 15.1 %collective-permute-start.17 = (bf16[256,1024]{1,0:T(8,128)(2,1)S(1)}, bf16[256,1024]{1,0:T(8,128)(2,1)S(1)}, u32[]{:S(2)}, u32[]{:S(2)}) collective-permute-start(bf16[256,1024]{1,0:T(8,128)(2,1)S(1)} %convolution_convert_fusion.1), channel_id=1, source_target_pairs={{0,2},{2,0},{4,6},{6,4},{8,14},{14,8},{10,12},{12,10},{1,3},{3,1},... | collective-permute-start | bytes 1572872 | tf_op jit(solution)/shard_map/ppermute | solution.py:22
  59.9 14.1 %collective-permute-start.7 = (bf16[128,2048]{1,0:T(8,128)(2,1)S(1)}, bf16[128,2048]{1,0:T(8,128)(2,1)S(1)}, u32[]{:S(2)}, u32[]{:S(2)}) collective-permute-start(bf16[128,2048]{1,0:T(8,128)(2,1)S(1)} %dynamic-slice_convert_fusion), channel_id=1, source_target_pairs={{0,6},{6,0},{2,4},{4,2},{8,10},{10,8},{12,14},{14,12},{1,7},{7,1},... | collective-permute-start | bytes 1572872 | tf_op jit(solution)/shard_map/ppermute | solution.py:22
  72.3 7.7 %collective-permute-start.18 = (bf16[128,1024]{1,0:T(8,128)(2,1)S(1)}, bf16[128,1024]{1,0:T(8,128)(2,1)S(1)}, u32[]{:S(2)}, u32[]{:S(2)}) collective-permute-start(bf16[128,1024]{1,0:T(8,128)(2,1)S(1)} %dynamic-slice_convert_fusion.1), channel_id=1, source_target_pairs={{0,6},{6,0},{2,4},{4,2},{8,10},{10,8},{12,14},{14,12},{1,7},{7,1},... | collective-permute-start | bytes 786440 | tf_op jit(solution)/shard_map/ppermute | solution.py:22
  74.2 12.0 %collective-permute-start.8 = (f32[64,2048]{1,0:T(8,128)S(1)}, f32[64,2048]{1,0:T(8,128)S(1)}, u32[]{:S(2)}, u32[]{:S(2)}) collective-permute-start(f32[64,2048]{1,0:T(8,128)S(1)} %constant_dynamic-slice_fusion.1), channel_id=1, source_target_pairs={{0,1},{1,0},{2,3},{3,2},{4,5},{5,4},{6,7},{7,6},{8,9},{9,8},{10,11... | collective-permute-start | bytes 1572872 | tf_op jit(solution)/shard_map/ppermute | solution.py:20
  80.1 11.7 %collective-permute-start.19 = (f32[64,1024]{1,0:T(8,128)S(1)}, f32[64,1024]{1,0:T(8,128)S(1)}, u32[]{:S(2)}, u32[]{:S(2)}) collective-permute-start(f32[64,1024]{1,0:T(8,128)S(1)} %constant_dynamic-slice_fusion), channel_id=1, source_target_pairs={{0,1},{1,0},{2,3},{3,2},{4,5},{5,4},{6,7},{7,6},{8,9},{9,8},{10,11... | collective-permute-start | bytes 786440 | tf_op jit(solution)/shard_map/ppermute | solution.py:20
  92.1 8.5 %collective-permute-start.22 = (bf16[64,2048]{1,0:T(8,128)(2,1)S(1)}, bf16[64,2048]{1,0:T(8,128)(2,1)S(1)}, u32[]{:S(2)}, u32[]{:S(2)}) collective-permute-start(bf16[64,2048]{1,0:T(8,128)(2,1)S(1)} %pad_maximum_fusion.8), channel_id=1, source_target_pairs={{0,1},{1,0},{2,3},{3,2},{4,5},{5,4},{6,7},{7,6},{8,9},{9,8},{10,11... | collective-permute-start | bytes 786440 | tf_op jit(solution)/shard_map/ppermute | solution.py:20
  93.8 6.1 %collective-permute-start.9 = (bf16[64,1024]{1,0:T(8,128)(2,1)S(1)}, bf16[64,1024]{1,0:T(8,128)(2,1)S(1)}, u32[]{:S(2)}, u32[]{:S(2)}) collective-permute-start(bf16[64,1024]{1,0:T(8,128)(2,1)S(1)} %get-tuple-element.32), channel_id=1, source_target_pairs={{0,1},{1,0},{2,3},{3,2},{4,5},{5,4},{6,7},{7,6},{8,9},{9,8},{10,11... | collective-permute-start | bytes 393224 | tf_op jit(solution)/shard_map/ppermute | solution.py:20
  100.0 10.5 %collective-permute-start.10 = (bf16[128,1024]{1,0:T(8,128)(2,1)S(1)}, bf16[128,1024]{1,0:T(8,128)(2,1)S(1)}, u32[]{:S(2)}, u32[]{:S(2)}) collective-permute-start(bf16[128,1024]{1,0:T(8,128)(2,1)S(1)} %maximum_select_fusion.5), channel_id=1, source_target_pairs={{0,6},{6,0},{2,4},{4,2},{8,10},{10,8},{12,14},{14,12},{1,7},{7,1},... | collective-permute-start | bytes 786440 | tf_op jit(solution)/shard_map/ppermute | solution.py:22
  100.6 16.1 %collective-permute-start.23 = (bf16[128,2048]{1,0:T(8,128)(2,1)S(1)}, bf16[128,2048]{1,0:T(8,128)(2,1)S(1)}, u32[]{:S(2)}, u32[]{:S(2)}) collective-permute-start(bf16[128,2048]{1,0:T(8,128)(2,1)S(1)} %maximum_select_fusion.4), channel_id=1, source_target_pairs={{0,6},{6,0},{2,4},{4,2},{8,10},{10,8},{12,14},{14,12},{1,7},{7,1},... | collective-permute-start | bytes 1572872 | tf_op jit(solution)/shard_map/ppermute | solution.py:22
  110.6 9.3 %collective-permute-start.20 = (bf16[256,1024]{1,0:T(8,128)(2,1)S(1)}, bf16[256,1024]{1,0:T(8,128)(2,1)S(1)}, u32[]{:S(2)}, u32[]{:S(2)}) collective-permute-start(bf16[256,1024]{1,0:T(8,128)(2,1)S(1)} %maximum_select_fusion.3), channel_id=1, source_target_pairs={{0,2},{2,0},{4,6},{6,4},{8,14},{14,8},{10,12},{12,10},{1,3},{3,1},... | collective-permute-start | bytes 1572872 | tf_op jit(solution)/shard_map/ppermute | solution.py:22
  110.7 14.8 %collective-permute-start.31 = (bf16[512,1024]{1,0:T(8,128)(2,1)S(1)}, bf16[512,1024]{1,0:T(8,128)(2,1)S(1)}, u32[]{:S(2)}, u32[]{:S(2)}) collective-permute-start(bf16[512,1024]{1,0:T(8,128)(2,1)S(1)} %constant_dynamic-update-slice_fusion.8), channel_id=1, source_target_pairs={{0,8},{8,0},{1,9},{9,1},{2,10},{10,2},{3,11},{11,3},{4,12},{12,4},... | collective-permute-start | bytes 3145736 | tf_op jit(solution)/shard_map/ppermute | solution.py:15
  117.0 14.9 %collective-permute-start.24 = (bf16[256,2048]{1,0:T(8,128)(2,1)S(1)}, bf16[256,2048]{1,0:T(8,128)(2,1)S(1)}, u32[]{:S(2)}, u32[]{:S(2)}) collective-permute-start(bf16[256,2048]{1,0:T(8,128)(2,1)S(1)} %maximum_select_fusion.2), channel_id=1, source_target_pairs={{0,2},{2,0},{4,6},{6,4},{8,14},{14,8},{10,12},{12,10},{1,3},{3,1},... | collective-permute-start | bytes 3145736 | tf_op jit(solution)/shard_map/ppermute | solution.py:22
  120.5 29.3 %collective-permute-start.28 = (bf16[512,1024]{1,0:T(8,128)(2,1)S(1)}, bf16[512,1024]{1,0:T(8,128)(2,1)S(1)}, u32[]{:S(2)}, u32[]{:S(2)}) collective-permute-start(bf16[512,1024]{1,0:T(8,128)(2,1)S(1)} %constant_dynamic-update-slice_fusion), channel_id=1, source_target_pairs={{0,8},{8,0},{1,9},{9,1},{2,10},{10,2},{3,11},{11,3},{4,12},{12,4},... | collective-permute-start | bytes 3145736 | tf_op jit(solution)/shard_map/ppermute | solution.py:15
  122.3 16.6 %collective-permute-start.21 = (bf16[256,1024]{1,0:T(8,128)(2,1)S(1)}, bf16[256,1024]{1,0:T(8,128)(2,1)S(1)}, u32[]{:S(2)}, u32[]{:S(2)}) collective-permute-start(bf16[256,1024]{1,0:T(8,128)(2,1)S(1)} %slice.197), channel_id=1, source_target_pairs={{0,16},{16,0},{1,17},{17,1},{2,18},{18,2},{3,19},{19,3},{4,20},{20... | collective-permute-start | bytes 1572872 | tf_op jit(solution)/shard_map/ppermute | solution.py:15
  135.4 13.9 %collective-permute-start.25 = (bf16[256,1024]{1,0:T(8,128)(2,1)S(1)}, bf16[256,1024]{1,0:T(8,128)(2,1)S(1)}, u32[]{:S(2)}, u32[]{:S(2)}) collective-permute-start(bf16[256,1024]{1,0:T(8,128)(2,1)S(1)} %slice.196), channel_id=1, source_target_pairs={{0,16},{16,0},{1,17},{17,1},{2,18},{18,2},{3,19},{19,3},{4,20},{20... | collective-permute-start | bytes 1572872 | tf_op jit(solution)/shard_map/ppermute | solution.py:15
  138.9 10.8 %collective-permute-start.29 = (bf16[512,1024]{1,0:T(8,128)(2,1)S(1)}, bf16[512,1024]{1,0:T(8,128)(2,1)S(1)}, u32[]{:S(2)}, u32[]{:S(2)}) collective-permute-start(bf16[512,1024]{1,0:T(8,128)(2,1)S(1)} %slice.137), channel_id=1, source_target_pairs={{0,8},{8,0},{1,9},{9,1},{2,10},{10,2},{3,11},{11,3},{4,12},{12,4},... | collective-permute-start | bytes 3145736 | tf_op jit(solution)/shard_map/ppermute | solution.py:15
  149.7 10.2 %collective-permute-start.27 = (bf16[128,2048]{1,0:T(8,128)(2,1)S(1)}, bf16[128,2048]{1,0:T(8,128)(2,1)S(1)}, u32[]{:S(2)}, u32[]{:S(2)}) collective-permute-start(bf16[128,2048]{1,0:T(8,128)(2,1)S(1)} %slice.135), channel_id=1, source_target_pairs={{0,192},{8,72},{32,224},{40,104},{64,0},{72,136},{96,32},{104,168}... | collective-permute-start | bytes 1572872 | tf_op jit(solution)/shard_map/ppermute | solution.py:39
  160.0 15.8 %collective-permute-start.32 = (bf16[64,2048]{1,0:T(8,128)(2,1)S(1)}, bf16[64,2048]{1,0:T(8,128)(2,1)S(1)}, u32[]{:S(2)}, u32[]{:S(2)}) collective-permute-start(bf16[64,2048]{1,0:T(8,128)(2,1)S(1)} %fusion.4), channel_id=1, source_target_pairs={{0,224},{8,40},{32,0},{40,72},{64,32},{72,104},{96,64},{104,136},{... | collective-permute-start | bytes 786440 | tf_op jit(solution)/shard_map/ppermute | solution.py:39
  169.9 9.0 %collective-permute-start.26 = (bf16[32,2048]{1,0:T(8,128)(2,1)S(1)}, bf16[32,2048]{1,0:T(8,128)(2,1)S(1)}, u32[]{:S(2)}, u32[]{:S(2)}) collective-permute-start(bf16[32,2048]{1,0:T(8,128)(2,1)S(1)} %slice.134), channel_id=1, source_target_pairs={{0,128},{8,136},{32,160},{40,168},{64,192},{72,200},{96,224},{104,... | collective-permute-start | bytes 393224 | tf_op jit(solution)/shard_map/ppermute | solution.py:39
  (7 other events, 56.9 us)
where the time goes:
time: 181 us; the launch traced here: 180 us
  waiting for transfers between devices  99.7 us (55%)
  starting transfers between devices  55.5 us (31%)
  matrix products  13 us (7%)
  other arithmetic  6.74 us (4%)
  local copies, waits for them, and re-layouts  3.5 us (2%)
    ppermute x8, waiting for transfers between devices, across(): return lax.ppermute(value, ('core', 'x'), pairs)  36.4 us
    ppermute x9, starting transfers between devices, along_z(): return lax.ppermute(value, ('z', 'core'), pairs)  25.7 us
    ppermute x9, waiting for transfers between devices, along_z(): return lax.ppermute(value, ('z', 'core'), pairs)  24.3 us
    ppermute x13, waiting for transfers between devices, swap(): return lax.ppermute(value, axis, SWAP)  24 us
    ppermute x4, waiting for transfers between devices, across(): return lax.ppermute(value, 'yl', SWAP)  15 us
    ppermute x13, starting transfers between devices, swap(): return lax.ppermute(value, axis, SWAP)  15 us
    ppermute x8, starting transfers between devices, across(): return lax.ppermute(value, ('core', 'x'), pairs)  8.25 us
    ppermute x4, starting transfers between devices, across(): return lax.ppermute(value, 'yl', SWAP)  6.56 us
  transfers between devices with their start and end apart: 34, of which 18 were waited for; matrix products, arithmetic and copies ran while one was open for 10% of the time, Pallas kernels for 0%

commit v1 on v0

--- a/solution.py
+++ b/solution.py
@@ -89,13 +89,14 @@
     return keep, sent
 
 
-def gather_dp(share, bits, first=None):
+def gather_dp(share, bits, **first):
     for dim in "cqp":
+        last = share
         other = across(share, dim)
-        if first is not None and dim == "q":
-            other = after(other, first)
+        if dim in first:
+            other = after(other, first[dim])
         share = jnp.where(bits[dim][2], join(share, other), join(other, share))
-    return share
+    return share, last
 
 
 def body(tokens, gate_weight, up_weight, down_weight, cotangent):
@@ -127,8 +128,8 @@
     pre = jnp.concatenate(
         [pre_gate[:, :width], pre_up[:, :width], pre_gate[:, width:], pre_up[:, width:]], axis=1
     )
-    hidden_half = gather_dp(hidden, bits, pre)
-    pre_half = gather_dp(pre, bits)
+    pre_half, last = gather_dp(pre, bits)
+    hidden_half, _ = gather_dp(hidden, bits, q=pre, p=last)
 
     token_other, cot_other = swap(token_half, "core"), swap(cot_half, "core")
     hidden_other = swap(hidden_half[:, width:], "core")

time: 181 us -> 181 us (level)
  no operation moved by 1% of the time
where the time goes in v1:
time: 181 us; the launch traced here: 180 us
  waiting for transfers between devices  99.7 us (55%)
  starting transfers between devices  55.5 us (31%)
  matrix products  13 us (7%)
  other arithmetic  6.74 us (4%)
  local copies, waits for them, and re-layouts  3.5 us (2%)
    ppermute x8, waiting for transfers between devices, across(): return lax.ppermute(value, ('core', 'x'), pairs)  36.4 us
    ppermute x9, starting transfers between devices, along_z(): return lax.ppermute(value, ('z', 'core'), pairs)  25.7 us
    ppermute x9, waiting for transfers between devices, along_z(): return lax.ppermute(value, ('z', 'core'), pairs)  24.3 us
    ppermute x13, waiting for transfers between devices, swap(): return lax.ppermute(value, axis, SWAP)  24 us
    ppermute x4, waiting for transfers between devices, across(): return lax.ppermute(value, 'yl', SWAP)  15 us
    ppermute x13, starting transfers between devices, swap(): return lax.ppermute(value, axis, SWAP)  15 us
    ppermute x8, starting transfers between devices, across(): return lax.ppermute(value, ('core', 'x'), pairs)  8.25 us
    ppermute x4, starting transfers between devices, across(): return lax.ppermute(value, 'yl', SWAP)  6.56 us
  transfers between devices with their start and end apart: 34, of which 18 were waited for; matrix products, arithmetic and copies ran while one was open for 10% of the time, Pallas kernels for 0%

profile of v1, /device:TPU:6, one launch (start us, length us, event | category | flops | bytes accessed | tf_op | source)
XLA Modules:
  0.0 179.6 jit_solution(718752695204144181)
XLA Ops:
  0.7 3.3 %pad_maximum_fusion.1 = bf16[1024,1024]{1,0:T(8,128)(2,1)} fusion(bf16[1024,512]{1,0:T(8,128)(2,1)} %param.7, bf16[1024,512]{1,0:T(8,128)(2,1)} %param.6), kind=kLoop, calls=%fused_computation.9 | loop fusion | flops 4194304 | bytes 4194304 | tf_op jit(solution)/shard_map/concatenate | solution.py:110
  4.4 7.2 %collective-permute-start.3 = (bf16[32,1024]{1,0:T(8,128)(2,1)S(1)}, bf16[32,1024]{1,0:T(8,128)(2,1)S(1)}, u32[]{:S(2)}, u32[]{:S(2)}) collective-permute-start(bf16[32,1024]{1,0:T(8,128)(2,1)S(1)} %copy-done.3), channel_id=1, source_target_pairs={{0,128},{8,136},{32,160},{40,168},{64,192},{72,200},{96,224},{104,... | collective-permute-start | bytes 196616 | tf_op jit(solution)/shard_map/ppermute | solution.py:39
  13.4 5.0 %collective-permute-done.1 = bf16[64,1024]{1,0:T(8,128)(2,1)S(1)} collective-permute-done((bf16[64,1024]{1,0:T(8,128)(2,1)S(1)}, bf16[64,1024]{1,0:T(8,128)(2,1)S(1)}, u32[]{:S(2)}, u32[]{:S(2)}) %collective-permute-start.1) | collective-permute-done | bytes 131104 | tf_op jit(solution)/shard_map/ppermute | solution.py:39
  19.2 3.9 %collective-permute-start.14 = (bf16[32,1024]{1,0:T(8,128)(2,1)S(1)}, bf16[32,1024]{1,0:T(8,128)(2,1)S(1)}, u32[]{:S(2)}, u32[]{:S(2)}) collective-permute-start(bf16[32,1024]{1,0:T(8,128)(2,1)S(1)} %copy-done.4), channel_id=1, source_target_pairs={{0,128},{8,136},{32,160},{40,168},{64,192},{72,200},{96,224},{104,... | collective-permute-start | bytes 196616 | tf_op jit(solution)/shard_map/ppermute | solution.py:39
  23.6 6.3 %collective-permute-done.2 = bf16[128,1024]{1,0:T(8,128)(2,1)S(1)} collective-permute-done((bf16[128,1024]{1,0:T(8,128)(2,1)S(1)}, bf16[128,1024]{1,0:T(8,128)(2,1)S(1)}, u32[]{:S(2)}, u32[]{:S(2)}) %collective-permute-start.2) | collective-permute-done | bytes 262176 | tf_op jit(solution)/shard_map/ppermute | solution.py:39
  30.0 3.3 %collective-permute-start.4 = (bf16[256,1024]{1,0:T(8,128)(2,1)S(1)}, bf16[256,1024]{1,0:T(8,128)(2,1)S(1)}, u32[]{:S(2)}, u32[]{:S(2)}) collective-permute-start(bf16[256,1024]{1,0:T(8,128)(2,1)S(1)} %pad_maximum_fusion.2), channel_id=1, source_target_pairs={{0,16},{16,0},{1,17},{17,1},{2,18},{18,2},{3,19},{19,3},{4,20},{20... | collective-permute-start | bytes 1572872 | tf_op jit(solution)/shard_map/ppermute | solution.py:15
  34.1 7.9 %collective-permute-done.4 = bf16[256,1024]{1,0:T(8,128)(2,1)S(1)} collective-permute-done((bf16[256,1024]{1,0:T(8,128)(2,1)S(1)}, bf16[256,1024]{1,0:T(8,128)(2,1)S(1)}, u32[]{:S(2)}, u32[]{:S(2)}) %collective-permute-start.4) | collective-permute-done | bytes 524320 | tf_op jit(solution)/shard_map/ppermute | solution.py:15
  44.5 3.3 %collective-permute-start.15 = (bf16[256,1024]{1,0:T(8,128)(2,1)S(1)}, bf16[256,1024]{1,0:T(8,128)(2,1)S(1)}, u32[]{:S(2)}, u32[]{:S(2)}) collective-permute-start(bf16[256,1024]{1,0:T(8,128)(2,1)S(1)} %pad_maximum_fusion.3), channel_id=1, source_target_pairs={{0,16},{16,0},{1,17},{17,1},{2,18},{18,2},{3,19},{19,3},{4,20},{20... | collective-permute-start | bytes 1572872 | tf_op jit(solution)/shard_map/ppermute | solution.py:15
  47.9 7.5 %collective-permute-done.15 = bf16[256,1024]{1,0:T(8,128)(2,1)S(1)} collective-permute-done((bf16[256,1024]{1,0:T(8,128)(2,1)S(1)}, bf16[256,1024]{1,0:T(8,128)(2,1)S(1)}, u32[]{:S(2)}, u32[]{:S(2)}) %collective-permute-start.15) | collective-permute-done | bytes 524320 | tf_op jit(solution)/shard_map/ppermute | solution.py:15
  60.7 10.7 %collective-permute-done.17 = bf16[256,1024]{1,0:T(8,128)(2,1)S(1)} collective-permute-done((bf16[256,1024]{1,0:T(8,128)(2,1)S(1)}, bf16[256,1024]{1,0:T(8,128)(2,1)S(1)}, u32[]{:S(2)}, u32[]{:S(2)}) %collective-permute-start.17) | collective-permute-done | bytes 524320 | tf_op jit(solution)/shard_map/ppermute | solution.py:22
  72.3 1.7 collective-permute-start.18
  74.2 2.2 %collective-permute-start.8 = (f32[64,2048]{1,0:T(8,128)S(1)}, f32[64,2048]{1,0:T(8,128)S(1)}, u32[]{:S(2)}, u32[]{:S(2)}) collective-permute-start(f32[64,2048]{1,0:T(8,128)S(1)} %constant_dynamic-slice_fusion.1), channel_id=1, source_target_pairs={{0,1},{1,0},{2,3},{3,2},{4,5},{5,4},{6,7},{7,6},{8,9},{9,8},{10,11... | collective-permute-start | bytes 1572872 | tf_op jit(solution)/shard_map/ppermute | solution.py:20
  76.5 3.5 %collective-permute-done.18 = bf16[128,1024]{1,0:T(8,128)(2,1)S(1)} collective-permute-done((bf16[128,1024]{1,0:T(8,128)(2,1)S(1)}, bf16[128,1024]{1,0:T(8,128)(2,1)S(1)}, u32[]{:S(2)}, u32[]{:S(2)}) %collective-permute-start.18) | collective-permute-done | bytes 262176 | tf_op jit(solution)/shard_map/ppermute | solution.py:22
  80.1 2.2 %collective-permute-start.19 = (f32[64,1024]{1,0:T(8,128)S(1)}, f32[64,1024]{1,0:T(8,128)S(1)}, u32[]{:S(2)}, u32[]{:S(2)}) collective-permute-start(f32[64,1024]{1,0:T(8,128)S(1)} %constant_dynamic-slice_fusion), channel_id=1, source_target_pairs={{0,1},{1,0},{2,3},{3,2},{4,5},{5,4},{6,7},{7,6},{8,9},{9,8},{10,11... | collective-permute-start | bytes 786440 | tf_op jit(solution)/shard_map/ppermute | solution.py:20
  82.3 3.9 %collective-permute-done.8 = f32[64,2048]{1,0:T(8,128)S(1)} collective-permute-done((f32[64,2048]{1,0:T(8,128)S(1)}, f32[64,2048]{1,0:T(8,128)S(1)}, u32[]{:S(2)}, u32[]{:S(2)}) %collective-permute-start.8) | collective-permute-done | bytes 524320 | tf_op jit(solution)/shard_map/ppermute | solution.py:20
  86.5 5.4 %collective-permute-done.19 = f32[64,1024]{1,0:T(8,128)S(1)} collective-permute-done((f32[64,1024]{1,0:T(8,128)S(1)}, f32[64,1024]{1,0:T(8,128)S(1)}, u32[]{:S(2)}, u32[]{:S(2)}) %collective-permute-start.19) | collective-permute-done | bytes 262176 | tf_op jit(solution)/shard_map/ppermute | solution.py:20
  92.1 1.8 collective-permute-start.21
  94.2 5.8 %collective-permute-done.9 = bf16[64,1024]{1,0:T(8,128)(2,1)S(1)} collective-permute-done((bf16[64,1024]{1,0:T(8,128)(2,1)S(1)}, bf16[64,1024]{1,0:T(8,128)(2,1)S(1)}, u32[]{:S(2)}, u32[]{:S(2)}) %collective-permute-start.9) | collective-permute-done | bytes 131104 | tf_op jit(solution)/shard_map/ppermute | solution.py:20
  100.6 2.9 %collective-permute-start.22 = (bf16[128,2048]{1,0:T(8,128)(2,1)S(1)}, bf16[128,2048]{1,0:T(8,128)(2,1)S(1)}, u32[]{:S(2)}, u32[]{:S(2)}) collective-permute-start(bf16[128,2048]{1,0:T(8,128)(2,1)S(1)} %maximum_select_fusion.4), channel_id=1, source_target_pairs={{0,6},{6,0},{2,4},{4,2},{8,10},{10,8},{12,14},{14,12},{1,7},{7,1},... | collective-permute-start | bytes 1572872 | tf_op jit(solution)/shard_map/ppermute | solution.py:22
  103.5 7.0 %collective-permute-done.10 = bf16[128,1024]{1,0:T(8,128)(2,1)S(1)} collective-permute-done((bf16[128,1024]{1,0:T(8,128)(2,1)S(1)}, bf16[128,1024]{1,0:T(8,128)(2,1)S(1)}, u32[]{:S(2)}, u32[]{:S(2)}) %collective-permute-start.10) | collective-permute-done | bytes 262176 | tf_op jit(solution)/shard_map/ppermute | solution.py:22
  110.8 5.9 %collective-permute-done.22 = bf16[128,2048]{1,0:T(8,128)(2,1)S(1)} collective-permute-done((bf16[128,2048]{1,0:T(8,128)(2,1)S(1)}, bf16[128,2048]{1,0:T(8,128)(2,1)S(1)}, u32[]{:S(2)}, u32[]{:S(2)}) %collective-permute-start.22) | collective-permute-done | bytes 524320 | tf_op jit(solution)/shard_map/ppermute | solution.py:22
  117.1 2.8 %collective-permute-done.20 = bf16[256,1024]{1,0:T(8,128)(2,1)S(1)} collective-permute-done((bf16[256,1024]{1,0:T(8,128)(2,1)S(1)}, bf16[256,1024]{1,0:T(8,128)(2,1)S(1)}, u32[]{:S(2)}, u32[]{:S(2)}) %collective-permute-start.20) | collective-permute-done | bytes 524320 | tf_op jit(solution)/shard_map/ppermute | solution.py:22
  122.3 3.2 %collective-permute-start.23 = (bf16[256,1024]{1,0:T(8,128)(2,1)S(1)}, bf16[256,1024]{1,0:T(8,128)(2,1)S(1)}, u32[]{:S(2)}, u32[]{:S(2)}) collective-permute-start(bf16[256,1024]{1,0:T(8,128)(2,1)S(1)} %slice.197), channel_id=1, source_target_pairs={{0,16},{16,0},{1,17},{17,1},{2,18},{18,2},{3,19},{19,3},{4,20},{20... | collective-permute-start | bytes 1572872 | tf_op jit(solution)/shard_map/ppermute | solution.py:15
  126.3 5.6 %collective-permute-done.24 = bf16[256,2048]{1,0:T(8,128)(2,1)S(1)} collective-permute-done((bf16[256,2048]{1,0:T(8,128)(2,1)S(1)}, bf16[256,2048]{1,0:T(8,128)(2,1)S(1)}, u32[]{:S(2)}, u32[]{:S(2)}) %collective-permute-start.24) | collective-permute-done | bytes 1048608 | tf_op jit(solution)/shard_map/ppermute | solution.py:22
  133.0 2.4 %fusion.26 = f32[512,1024]{1,0:T(8,128)S(1)} fusion(bf16[512,2048]{1,0:T(8,128)(2,1)S(1)} %maximum_select_fusion, bf16[1024,2048]{1,0:T(8,128)(2,1)S(1)} %constant_dynamic-update-slice_fusion.5), kind=kOutput, calls=%fused_computation.85 | convolution fusion | flops 2147483648 | bytes 8388608 | tf_op jit(solution)/shard_map/dot_general | solution.py:34
  135.4 3.5 %collective-permute-start.25 = (bf16[256,1024]{1,0:T(8,128)(2,1)S(1)}, bf16[256,1024]{1,0:T(8,128)(2,1)S(1)}, u32[]{:S(2)}, u32[]{:S(2)}) collective-permute-start(bf16[256,1024]{1,0:T(8,128)(2,1)S(1)} %slice.196), channel_id=1, source_target_pairs={{0,16},{16,0},{1,17},{17,1},{2,18},{18,2},{3,19},{19,3},{4,20},{20... | collective-permute-start | bytes 1572872 | tf_op jit(solution)/shard_map/ppermute | solution.py:15
  139.1 1.7 add_convert_fusion.1
  140.8 8.5 %collective-permute-done.25 = bf16[256,1024]{1,0:T(8,128)(2,1)S(1)} collective-permute-done((bf16[256,1024]{1,0:T(8,128)(2,1)S(1)}, bf16[256,1024]{1,0:T(8,128)(2,1)S(1)}, u32[]{:S(2)}, u32[]{:S(2)}) %collective-permute-start.25) | collective-permute-done | bytes 524320 | tf_op jit(solution)/shard_map/ppermute | solution.py:15
  152.5 7.3 %collective-permute-done.27 = bf16[128,2048]{1,0:T(8,128)(2,1)S(1)} collective-permute-done((bf16[128,2048]{1,0:T(8,128)(2,1)S(1)}, bf16[128,2048]{1,0:T(8,128)(2,1)S(1)}, u32[]{:S(2)}, u32[]{:S(2)}) %collective-permute-start.27) | collective-permute-done | bytes 524320 | tf_op jit(solution)/shard_map/ppermute | solution.py:39
  160.0 9.9 %collective-permute-start.32 = (bf16[64,2048]{1,0:T(8,128)(2,1)S(1)}, bf16[64,2048]{1,0:T(8,128)(2,1)S(1)}, u32[]{:S(2)}, u32[]{:S(2)}) collective-permute-start(bf16[64,2048]{1,0:T(8,128)(2,1)S(1)} %fusion.4), channel_id=1, source_target_pairs={{0,224},{8,40},{32,0},{40,72},{64,32},{72,104},{96,64},{104,136},{... | collective-permute-start | bytes 786440 | tf_op jit(solution)/shard_map/ppermute | solution.py:39
  169.9 1.7 collective-permute-start.26
  171.6 4.3 %collective-permute-done.32 = bf16[64,2048]{1,0:T(8,128)(2,1)S(1)} collective-permute-done((bf16[64,2048]{1,0:T(8,128)(2,1)S(1)}, bf16[64,2048]{1,0:T(8,128)(2,1)S(1)}, u32[]{:S(2)}, u32[]{:S(2)}) %collective-permute-start.32) | collective-permute-done | bytes 262176 | tf_op jit(solution)/shard_map/ppermute | solution.py:39
  (112 shorter events, 27.0 us)
Async XLA Ops:
  3.9 38.1 %collective-permute-start.5 = (bf16[1024,1024]{1,0:T(8,128)(2,1)}, bf16[1024,1024]{1,0:T(8,128)(2,1)S(1)}, u32[]{:S(2)}, u32[]{:S(2)}) collective-permute-start(bf16[1024,1024]{1,0:T(8,128)(2,1)} %pad_maximum_fusion.1), channel_id=1, source_target_pairs={{0,8},{8,0},{1,9},{9,1},{2,10},{10,2},{3,11},{11,3},{4,12},{12,4},... | collective-permute-start | bytes 6291464 | tf_op jit(solution)/shard_map/ppermute | solution.py:15
  3.9 8.2 %collective-permute-start = (bf16[32,1024]{1,0:T(8,128)(2,1)S(1)}, bf16[32,1024]{1,0:T(8,128)(2,1)S(1)}, u32[]{:S(2)}, u32[]{:S(2)}) collective-permute-start(bf16[32,1024]{1,0:T(8,128)(2,1)S(1)} %copy-done.3), channel_id=1, source_target_pairs={{0,8},{8,0},{1,9},{9,1},{2,10},{10,2},{3,11},{11,3},{4,12},{12,4},... | collective-permute-start | bytes 196616 | tf_op jit(solution)/shard_map/ppermute | solution.py:15
  4.4 18.7 %collective-permute-start.3 = (bf16[32,1024]{1,0:T(8,128)(2,1)S(1)}, bf16[32,1024]{1,0:T(8,128)(2,1)S(1)}, u32[]{:S(2)}, u32[]{:S(2)}) collective-permute-start(bf16[32,1024]{1,0:T(8,128)(2,1)S(1)} %copy-done.3), channel_id=1, source_target_pairs={{0,128},{8,136},{32,160},{40,168},{64,192},{72,200},{96,224},{104,... | collective-permute-start | bytes 196616 | tf_op jit(solution)/shard_map/ppermute | solution.py:39
  11.6 36.2 %collective-permute-start.16 = (bf16[512,1024]{1,0:T(8,128)(2,1)}, bf16[512,1024]{1,0:T(8,128)(2,1)S(1)}, u32[]{:S(2)}, u32[]{:S(2)}) collective-permute-start(bf16[512,1024]{1,0:T(8,128)(2,1)} %param.8), channel_id=1, source_target_pairs={{0,8},{8,0},{1,9},{9,1},{2,10},{10,2},{3,11},{11,3},{4,12},{12,4},... | collective-permute-start | bytes 3145736 | tf_op jit(solution)/shard_map/ppermute | solution.py:15
  11.6 7.6 %collective-permute-start.11 = (bf16[32,1024]{1,0:T(8,128)(2,1)S(1)}, bf16[32,1024]{1,0:T(8,128)(2,1)S(1)}, u32[]{:S(2)}, u32[]{:S(2)}) collective-permute-start(bf16[32,1024]{1,0:T(8,128)(2,1)S(1)} %copy-done.4), channel_id=1, source_target_pairs={{0,8},{8,0},{1,9},{9,1},{2,10},{10,2},{3,11},{11,3},{4,12},{12,4},... | collective-permute-start | bytes 196616 | tf_op jit(solution)/shard_map/ppermute | solution.py:15
  12.2 6.3 %collective-permute-start.1 = (bf16[64,1024]{1,0:T(8,128)(2,1)S(1)}, bf16[64,1024]{1,0:T(8,128)(2,1)S(1)}, u32[]{:S(2)}, u32[]{:S(2)}) collective-permute-start(bf16[64,1024]{1,0:T(8,128)(2,1)S(1)} %pad_maximum_fusion.9), channel_id=1, source_target_pairs={{0,32},{8,232},{32,64},{40,8},{64,96},{72,40},{96,128},{104,72},{1... | collective-permute-start | bytes 393224 | tf_op jit(solution)/shard_map/ppermute | solution.py:39
  18.4 11.5 %collective-permute-start.2 = (bf16[128,1024]{1,0:T(8,128)(2,1)S(1)}, bf16[128,1024]{1,0:T(8,128)(2,1)S(1)}, u32[]{:S(2)}, u32[]{:S(2)}) collective-permute-start(bf16[128,1024]{1,0:T(8,128)(2,1)S(1)} %pad_maximum_fusion.4), channel_id=1, source_target_pairs={{0,64},{8,200},{32,96},{40,232},{64,128},{72,8},{96,160},{104,40},... | collective-permute-start | bytes 786440 | tf_op jit(solution)/shard_map/ppermute | solution.py:39
  19.2 25.3 %collective-permute-start.14 = (bf16[32,1024]{1,0:T(8,128)(2,1)S(1)}, bf16[32,1024]{1,0:T(8,128)(2,1)S(1)}, u32[]{:S(2)}, u32[]{:S(2)}) collective-permute-start(bf16[32,1024]{1,0:T(8,128)(2,1)S(1)} %copy-done.4), channel_id=1, source_target_pairs={{0,128},{8,136},{32,160},{40,168},{64,192},{72,200},{96,224},{104,... | collective-permute-start | bytes 196616 | tf_op jit(solution)/shard_map/ppermute | solution.py:39
  23.1 10.1 %collective-permute-start.12 = (bf16[64,1024]{1,0:T(8,128)(2,1)S(1)}, bf16[64,1024]{1,0:T(8,128)(2,1)S(1)}, u32[]{:S(2)}, u32[]{:S(2)}) collective-permute-start(bf16[64,1024]{1,0:T(8,128)(2,1)S(1)} %pad_maximum_fusion.10), channel_id=1, source_target_pairs={{0,32},{8,232},{32,64},{40,8},{64,96},{72,40},{96,128},{104,72},{1... | collective-permute-start | bytes 393224 | tf_op jit(solution)/shard_map/ppermute | solution.py:39
  30.0 12.0 %collective-permute-start.4 = (bf16[256,1024]{1,0:T(8,128)(2,1)S(1)}, bf16[256,1024]{1,0:T(8,128)(2,1)S(1)}, u32[]{:S(2)}, u32[]{:S(2)}) collective-permute-start(bf16[256,1024]{1,0:T(8,128)(2,1)S(1)} %pad_maximum_fusion.2), channel_id=1, source_target_pairs={{0,16},{16,0},{1,17},{17,1},{2,18},{18,2},{3,19},{19,3},{4,20},{20... | collective-permute-start | bytes 1572872 | tf_op jit(solution)/shard_map/ppermute | solution.py:15
  33.3 11.2 %collective-permute-start.13 = (bf16[128,1024]{1,0:T(8,128)(2,1)S(1)}, bf16[128,1024]{1,0:T(8,128)(2,1)S(1)}, u32[]{:S(2)}, u32[]{:S(2)}) collective-permute-start(bf16[128,1024]{1,0:T(8,128)(2,1)S(1)} %pad_maximum_fusion.7), channel_id=1, source_target_pairs={{0,64},{8,200},{32,96},{40,232},{64,128},{72,8},{96,160},{104,40},... | collective-permute-start | bytes 786440 | tf_op jit(solution)/shard_map/ppermute | solution.py:39
  43.6 14.9 %collective-permute-start.6 = (bf16[256,2048]{1,0:T(8,128)(2,1)S(1)}, bf16[256,2048]{1,0:T(8,128)(2,1)S(1)}, u32[]{:S(2)}, u32[]{:S(2)}) collective-permute-start(bf16[256,2048]{1,0:T(8,128)(2,1)S(1)} %convolution_convert_fusion), channel_id=1, source_target_pairs={{0,2},{2,0},{4,6},{6,4},{8,14},{14,8},{10,12},{12,10},{1,3},{3,1},... | collective-permute-start | bytes 3145736 | tf_op jit(solution)/shard_map/ppermute | solution.py:22
  44.5 11.0 %collective-permute-start.15 = (bf16[256,1024]{1,0:T(8,128)(2,1)S(1)}, bf16[256,1024]{1,0:T(8,128)(2,1)S(1)}, u32[]{:S(2)}, u32[]{:S(2)}) collective-permute-start(bf16[256,1024]{1,0:T(8,128)(2,1)S(1)} %pad_maximum_fusion.3), channel_id=1, source_target_pairs={{0,16},{16,0},{1,17},{17,1},{2,18},{18,2},{3,19},{19,3},{4,20},{20... | collective-permute-start | bytes 1572872 | tf_op jit(solution)/shard_map/ppermute | solution.py:15
  56.3 15.1 %collective-permute-start.17 = (bf16[256,1024]{1,0:T(8,128)(2,1)S(1)}, bf16[256,1024]{1,0:T(8,128)(2,1)S(1)}, u32[]{:S(2)}, u32[]{:S(2)}) collective-permute-start(bf16[256,1024]{1,0:T(8,128)(2,1)S(1)} %convolution_convert_fusion.1), channel_id=1, source_target_pairs={{0,2},{2,0},{4,6},{6,4},{8,14},{14,8},{10,12},{12,10},{1,3},{3,1},... | collective-permute-start | bytes 1572872 | tf_op jit(solution)/shard_map/ppermute | solution.py:22
  59.9 14.1 %collective-permute-start.7 = (bf16[128,2048]{1,0:T(8,128)(2,1)S(1)}, bf16[128,2048]{1,0:T(8,128)(2,1)S(1)}, u32[]{:S(2)}, u32[]{:S(2)}) collective-permute-start(bf16[128,2048]{1,0:T(8,128)(2,1)S(1)} %dynamic-slice_convert_fusion), channel_id=1, source_target_pairs={{0,6},{6,0},{2,4},{4,2},{8,10},{10,8},{12,14},{14,12},{1,7},{7,1},... | collective-permute-start | bytes 1572872 | tf_op jit(solution)/shard_map/ppermute | solution.py:22
  72.3 7.7 %collective-permute-start.18 = (bf16[128,1024]{1,0:T(8,128)(2,1)S(1)}, bf16[128,1024]{1,0:T(8,128)(2,1)S(1)}, u32[]{:S(2)}, u32[]{:S(2)}) collective-permute-start(bf16[128,1024]{1,0:T(8,128)(2,1)S(1)} %dynamic-slice_convert_fusion.1), channel_id=1, source_target_pairs={{0,6},{6,0},{2,4},{4,2},{8,10},{10,8},{12,14},{14,12},{1,7},{7,1},... | collective-permute-start | bytes 786440 | tf_op jit(solution)/shard_map/ppermute | solution.py:22
  74.2 12.0 %collective-permute-start.8 = (f32[64,2048]{1,0:T(8,128)S(1)}, f32[64,2048]{1,0:T(8,128)S(1)}, u32[]{:S(2)}, u32[]{:S(2)}) collective-permute-start(f32[64,2048]{1,0:T(8,128)S(1)} %constant_dynamic-slice_fusion.1), channel_id=1, source_target_pairs={{0,1},{1,0},{2,3},{3,2},{4,5},{5,4},{6,7},{7,6},{8,9},{9,8},{10,11... | collective-permute-start | bytes 1572872 | tf_op jit(solution)/shard_map/ppermute | solution.py:20
  80.1 11.7 %collective-permute-start.19 = (f32[64,1024]{1,0:T(8,128)S(1)}, f32[64,1024]{1,0:T(8,128)S(1)}, u32[]{:S(2)}, u32[]{:S(2)}) collective-permute-start(f32[64,1024]{1,0:T(8,128)S(1)} %constant_dynamic-slice_fusion), channel_id=1, source_target_pairs={{0,1},{1,0},{2,3},{3,2},{4,5},{5,4},{6,7},{7,6},{8,9},{9,8},{10,11... | collective-permute-start | bytes 786440 | tf_op jit(solution)/shard_map/ppermute | solution.py:20
  92.1 8.5 %collective-permute-start.21 = (bf16[64,2048]{1,0:T(8,128)(2,1)S(1)}, bf16[64,2048]{1,0:T(8,128)(2,1)S(1)}, u32[]{:S(2)}, u32[]{:S(2)}) collective-permute-start(bf16[64,2048]{1,0:T(8,128)(2,1)S(1)} %pad_maximum_fusion.8), channel_id=1, source_target_pairs={{0,1},{1,0},{2,3},{3,2},{4,5},{5,4},{6,7},{7,6},{8,9},{9,8},{10,11... | collective-permute-start | bytes 786440 | tf_op jit(solution)/shard_map/ppermute | solution.py:20
  93.8 6.1 %collective-permute-start.9 = (bf16[64,1024]{1,0:T(8,128)(2,1)S(1)}, bf16[64,1024]{1,0:T(8,128)(2,1)S(1)}, u32[]{:S(2)}, u32[]{:S(2)}) collective-permute-start(bf16[64,1024]{1,0:T(8,128)(2,1)S(1)} %get-tuple-element.33), channel_id=1, source_target_pairs={{0,1},{1,0},{2,3},{3,2},{4,5},{5,4},{6,7},{7,6},{8,9},{9,8},{10,11... | collective-permute-start | bytes 393224 | tf_op jit(solution)/shard_map/ppermute | solution.py:20
  100.0 10.5 %collective-permute-start.10 = (bf16[128,1024]{1,0:T(8,128)(2,1)S(1)}, bf16[128,1024]{1,0:T(8,128)(2,1)S(1)}, u32[]{:S(2)}, u32[]{:S(2)}) collective-permute-start(bf16[128,1024]{1,0:T(8,128)(2,1)S(1)} %maximum_select_fusion.5), channel_id=1, source_target_pairs={{0,6},{6,0},{2,4},{4,2},{8,10},{10,8},{12,14},{14,12},{1,7},{7,1},... | collective-permute-start | bytes 786440 | tf_op jit(solution)/shard_map/ppermute | solution.py:22
  100.6 16.1 %collective-permute-start.22 = (bf16[128,2048]{1,0:T(8,128)(2,1)S(1)}, bf16[128,2048]{1,0:T(8,128)(2,1)S(1)}, u32[]{:S(2)}, u32[]{:S(2)}) collective-permute-start(bf16[128,2048]{1,0:T(8,128)(2,1)S(1)} %maximum_select_fusion.4), channel_id=1, source_target_pairs={{0,6},{6,0},{2,4},{4,2},{8,10},{10,8},{12,14},{14,12},{1,7},{7,1},... | collective-permute-start | bytes 1572872 | tf_op jit(solution)/shard_map/ppermute | solution.py:22
  110.6 9.3 %collective-permute-start.20 = (bf16[256,1024]{1,0:T(8,128)(2,1)S(1)}, bf16[256,1024]{1,0:T(8,128)(2,1)S(1)}, u32[]{:S(2)}, u32[]{:S(2)}) collective-permute-start(bf16[256,1024]{1,0:T(8,128)(2,1)S(1)} %maximum_select_fusion.3), channel_id=1, source_target_pairs={{0,2},{2,0},{4,6},{6,4},{8,14},{14,8},{10,12},{12,10},{1,3},{3,1},... | collective-permute-start | bytes 1572872 | tf_op jit(solution)/shard_map/ppermute | solution.py:22
  110.7 14.8 %collective-permute-start.31 = (bf16[512,1024]{1,0:T(8,128)(2,1)S(1)}, bf16[512,1024]{1,0:T(8,128)(2,1)S(1)}, u32[]{:S(2)}, u32[]{:S(2)}) collective-permute-start(bf16[512,1024]{1,0:T(8,128)(2,1)S(1)} %constant_dynamic-update-slice_fusion.8), channel_id=1, source_target_pairs={{0,8},{8,0},{1,9},{9,1},{2,10},{10,2},{3,11},{11,3},{4,12},{12,4},... | collective-permute-start | bytes 3145736 | tf_op jit(solution)/shard_map/ppermute | solution.py:15
  117.0 14.9 %collective-permute-start.24 = (bf16[256,2048]{1,0:T(8,128)(2,1)S(1)}, bf16[256,2048]{1,0:T(8,128)(2,1)S(1)}, u32[]{:S(2)}, u32[]{:S(2)}) collective-permute-start(bf16[256,2048]{1,0:T(8,128)(2,1)S(1)} %maximum_select_fusion.1), channel_id=1, source_target_pairs={{0,2},{2,0},{4,6},{6,4},{8,14},{14,8},{10,12},{12,10},{1,3},{3,1},... | collective-permute-start | bytes 3145736 | tf_op jit(solution)/shard_map/ppermute | solution.py:22
  120.5 29.3 %collective-permute-start.28 = (bf16[512,1024]{1,0:T(8,128)(2,1)S(1)}, bf16[512,1024]{1,0:T(8,128)(2,1)S(1)}, u32[]{:S(2)}, u32[]{:S(2)}) collective-permute-start(bf16[512,1024]{1,0:T(8,128)(2,1)S(1)} %constant_dynamic-update-slice_fusion), channel_id=1, source_target_pairs={{0,8},{8,0},{1,9},{9,1},{2,10},{10,2},{3,11},{11,3},{4,12},{12,4},... | collective-permute-start | bytes 3145736 | tf_op jit(solution)/shard_map/ppermute | solution.py:15
  122.3 16.6 %collective-permute-start.23 = (bf16[256,1024]{1,0:T(8,128)(2,1)S(1)}, bf16[256,1024]{1,0:T(8,128)(2,1)S(1)}, u32[]{:S(2)}, u32[]{:S(2)}) collective-permute-start(bf16[256,1024]{1,0:T(8,128)(2,1)S(1)} %slice.197), channel_id=1, source_target_pairs={{0,16},{16,0},{1,17},{17,1},{2,18},{18,2},{3,19},{19,3},{4,20},{20... | collective-permute-start | bytes 1572872 | tf_op jit(solution)/shard_map/ppermute | solution.py:15
  135.4 13.9 %collective-permute-start.25 = (bf16[256,1024]{1,0:T(8,128)(2,1)S(1)}, bf16[256,1024]{1,0:T(8,128)(2,1)S(1)}, u32[]{:S(2)}, u32[]{:S(2)}) collective-permute-start(bf16[256,1024]{1,0:T(8,128)(2,1)S(1)} %slice.196), channel_id=1, source_target_pairs={{0,16},{16,0},{1,17},{17,1},{2,18},{18,2},{3,19},{19,3},{4,20},{20... | collective-permute-start | bytes 1572872 | tf_op jit(solution)/shard_map/ppermute | solution.py:15
  138.9 10.8 %collective-permute-start.29 = (bf16[512,1024]{1,0:T(8,128)(2,1)S(1)}, bf16[512,1024]{1,0:T(8,128)(2,1)S(1)}, u32[]{:S(2)}, u32[]{:S(2)}) collective-permute-start(bf16[512,1024]{1,0:T(8,128)(2,1)S(1)} %slice.137), channel_id=1, source_target_pairs={{0,8},{8,0},{1,9},{9,1},{2,10},{10,2},{3,11},{11,3},{4,12},{12,4},... | collective-permute-start | bytes 3145736 | tf_op jit(solution)/shard_map/ppermute | solution.py:15
  149.7 10.2 %collective-permute-start.27 = (bf16[128,2048]{1,0:T(8,128)(2,1)S(1)}, bf16[128,2048]{1,0:T(8,128)(2,1)S(1)}, u32[]{:S(2)}, u32[]{:S(2)}) collective-permute-start(bf16[128,2048]{1,0:T(8,128)(2,1)S(1)} %slice.135), channel_id=1, source_target_pairs={{0,192},{8,72},{32,224},{40,104},{64,0},{72,136},{96,32},{104,168}... | collective-permute-start | bytes 1572872 | tf_op jit(solution)/shard_map/ppermute | solution.py:39
  160.0 15.8 %collective-permute-start.32 = (bf16[64,2048]{1,0:T(8,128)(2,1)S(1)}, bf16[64,2048]{1,0:T(8,128)(2,1)S(1)}, u32[]{:S(2)}, u32[]{:S(2)}) collective-permute-start(bf16[64,2048]{1,0:T(8,128)(2,1)S(1)} %fusion.4), channel_id=1, source_target_pairs={{0,224},{8,40},{32,0},{40,72},{64,32},{72,104},{96,64},{104,136},{... | collective-permute-start | bytes 786440 | tf_op jit(solution)/shard_map/ppermute | solution.py:39
  169.9 9.0 %collective-permute-start.26 = (bf16[32,2048]{1,0:T(8,128)(2,1)S(1)}, bf16[32,2048]{1,0:T(8,128)(2,1)S(1)}, u32[]{:S(2)}, u32[]{:S(2)}) collective-permute-start(bf16[32,2048]{1,0:T(8,128)(2,1)S(1)} %slice.134), channel_id=1, source_target_pairs={{0,128},{8,136},{32,160},{40,168},{64,192},{72,200},{96,224},{104,... | collective-permute-start | bytes 393224 | tf_op jit(solution)/shard_map/ppermute | solution.py:39
  (7 other events, 56.9 us)
